TPU v7x, 512 devices: a whole 4x8x8 slice. The times are simulated.
512 devices in a mesh: dp: 64 (over y_hi, z, x), seq: 8 (over y_lo, core).
Axes of the slice: x: 4, y: 8 (y_hi: 2, y_lo: 4; y = y_hi * 4 + y_lo), z: 8, core: 2. Of those that a mesh axis runs over, the one named last changes fastest.
Arguments:
- features: bfloat16 [64, 1024, 768], P('dp', 'seq'), may hold values from -6 to 6
- conv_weight: bfloat16 [5, 768, 1536], P(None, 'dp', 'seq'), as said below
- conv_bias: float32 [1536], replicated, may hold values from -0.5 to 0.5
- norm_gain: float32 [1536], replicated, may hold values from 0.5 to 2
- qkv_weight: bfloat16 [1536, 2560], P('dp', 'seq'), as said below
Outputs:
- mixed: bfloat16 [64, 512, 1536], P('dp', 'seq')
Inputs may be any that keep to these rules, and one draw needn't show every extreme that they name: `conv_weight`: entries of order one over the square root of 3840. `qkv_weight`: entries of magnitude at most 10.5 over the square root of 1536.
All inputs are finite; a program needn't handle non-finite values.
Results may differ from a plain program's by a relative error of at most 0.02.
The roundings to bfloat16 on the way count: a program that leaves them out, or rounds other values in their place, can miss the bound.
Values may be sent and summed in bfloat16 or wider, within the bound.
A program may use at most 64 MiB of HBM per device.

v0:
```python
import jax
import jax.numpy as jnp
from jax import lax
from jax.sharding import PartitionSpec as P

HK = 64
HV = 192


def with_halo(block, sides, width):
    for axis, dim in sides:
        count = lax.axis_size(axis)
        forward = [(i, i + 1) for i in range(count - 1)]
        backward = [(target, source) for source, target in forward]
        low = lax.ppermute(
            lax.slice_in_dim(block, block.shape[dim] - width, None, axis=dim), axis, forward
        )
        high = lax.ppermute(lax.slice_in_dim(block, 0, width, axis=dim), axis, backward)
        block = jnp.concatenate([low, block, high], axis=dim)
    return block


def conv_piece(total, padded, piece):
    rows = total.shape[0]
    for tap in range(piece.shape[0]):
        total = total + jnp.dot(
            padded[tap : tap + rows], piece[tap], preferred_element_type=jnp.float32
        )
    return total


def finish_conv(total, bias):
    rows, cols = total.shape
    active = jax.nn.gelu(total + bias, approximate=True)
    return jnp.max(active.reshape(rows // 2, 2, cols), axis=1).astype(jnp.bfloat16)


def attend(query, keys, values):
    length = query.shape[0]
    block = min(512, length)
    scale = query.shape[1] ** (-0.5)
    blocks = query.reshape(length // block, block, query.shape[1])

    def one_block(rows):
        scores = jnp.dot(rows, keys.T, preferred_element_type=jnp.float32) * scale
        top = jnp.max(scores, axis=-1, keepdims=True)
        expo = jnp.exp(scores - top)
        probs = (expo / jnp.sum(expo, axis=-1, keepdims=True)).astype(jnp.bfloat16)
        return jnp.dot(probs, values, preferred_element_type=jnp.float32).astype(jnp.bfloat16)

    return lax.map(one_block, blocks).reshape(length, values.shape[1])


def shards(features, conv_weight, conv_bias, norm_gain, qkv_weight):
    seq_in = features[0]
    in_rows = seq_in.shape[0]
    half = conv_weight.shape[0] // 2
    padded = with_halo(seq_in, (("seq", 0),), half)
    columns = lax.all_gather(conv_weight, "seq", axis=2, tiled=True)
    empty = jnp.zeros((in_rows, columns.shape[2]), jnp.float32)
    total = conv_piece(empty, padded, lax.all_gather(columns, "dp", axis=1, tiled=True))
    pooled = finish_conv(total, conv_bias)
    whole = lax.all_gather(pooled, "seq", axis=0, tiled=True)
    values32 = whole.astype(jnp.float32)
    mean = jnp.mean(values32, axis=-1, keepdims=True)
    centred = values32 - mean
    var = jnp.mean(centred * centred, axis=-1, keepdims=True)
    normed = (centred / jnp.sqrt(var + 1e-05) * norm_gain).astype(jnp.bfloat16)
    qkv = jnp.dot(
        normed,
        lax.all_gather(qkv_weight, "dp", axis=0, tiled=True),
        preferred_element_type=jnp.float32,
    ).astype(jnp.bfloat16)
    width = 2 * HK + HV
    outputs = attend(qkv[:, 0:HK], qkv[:, HK : 2 * HK], qkv[:, 2 * HK : width])
    arrived = lax.all_to_all(outputs, "seq", split_axis=0, concat_axis=1, tiled=True)
    mixed = (pooled.astype(jnp.float32) + arrived.astype(jnp.float32)).astype(jnp.bfloat16)
    return mixed[None]


def solution(mesh):
    return jax.shard_map(
        shards,
        mesh=mesh,
        in_specs=(P("dp", "seq", None), P(None, "dp", "seq"), P(), P(), P("dp", "seq")),
        out_specs=P("dp", "seq", None),
        check_vma=False,
    )
```

profile of v0, /device:TPU:1, one launch (start us, length us, event | category | flops | bytes accessed | tf_op | source)
XLA Modules:
  0.0 639.3 jit_solution(1128909861396048516)
XLA Ops:
  6.5 0.0 all-gather.3.cloned.1.call-start
  6.5 1.0 copy.14
  7.6 34.2 %all_gather.12 = bf16[5,12,1536]{1,0,2:T(8,128)(2,1)S(1)} all-gather(bf16[5,12,192]{1,0,2:T(8,128)(2,1)S(1)} %copy.14), channel_id=1, replica_groups=mesh['dp'=64,'seq'=8] {'seq'}, dimensions={2}, use_global_device_ids=true | all-gather | bytes 207360 | tf_op jit(solution)/shard_map/all_gather | solution.py:59
  41.8 0.0 copy-start.2
  41.8 2.9 copy.15
  44.7 0.0 all-gather.3.cloned.1.call-update
  44.8 0.0 all-gather.5.cloned.1.call-start
  44.8 0.0 copy-done.2
  44.8 3.6 collective-permute-start
  48.4 1.9 collective-permute-start.1
  50.4 298.7 %all-gather.3.cloned.1.call-done = bf16[5,768,1536]{2,0,1:T(8,128)(2,1)} async-done(((bf16[5,12,1536]{2,0,1:T(8,128)(2,1)}), bf16[5,768,1536]{2,0,1:T(8,128)(2,1)}) %all-gather.3.cloned.1.call-update) | async-done | bytes 11796496 | tf_op jit(solution)/shard_map/all_gather | solution.py:61
  349.1 36.2 %fusion.39 = (bf16[1,768,1536]{2,0,1:T(2,128)(2,1)S(1)}, bf16[1,768,1536]{2,0,1:T(2,128)(2,1)S(1)}, bf16[1,768,1536]{2,0,1:T(2,128)(2,1)S(1)}, bf16[1,768,1536]{2,0,1:T(2,128)(2,1)S(1)}, bf16[1,768,1536]{2,0,1:T(2,128)(2,1)S(1)}) fusion(bf16[5,768,1536]{2,0,1:T(8,128)(2,1)} %all-gather.3.cloned.1.call-done), kind=kLoop, calls=%fused_computation.60 | loop fusion | bytes 23592960 | tf_op jit(solution)/shard_map/slice | solution.py:27
  385.4 0.5 fusion.9
  385.8 0.0 collective-permute-done
  385.9 0.5 fusion.10
  386.4 0.0 collective-permute-done.1
  386.4 0.5 fusion.8
  386.9 0.0 copy-start.4
  386.9 0.5 fusion.7
  387.4 0.2 copy-done.4
  387.6 0.0 copy-start.3
  387.6 0.7 fusion.23
  388.3 0.0 copy-start.5
  388.3 0.1 reshape.60
  388.5 1.7 reduce_max.19
  390.2 0.0 all-gather.5.cloned.1.call-update
  390.2 0.0 copy-done.3
  390.2 194.8 %all_gather.15 = bf16[1536,320]{1,0:T(8,128)(2,1)S(1)} all-gather(bf16[24,320]{1,0:T(8,128)(2,1)S(1)} %copy-done.3), channel_id=1, replica_groups=mesh['dp'=64,'seq'=8] {'dp'}, dimensions={0}, use_global_device_ids=true | all-gather | bytes 998400 | tf_op jit(solution)/shard_map/all_gather | solution.py:71
  585.0 0.0 all-gather.5.cloned.1.call-done
  585.0 0.0 copy-start
  585.0 1.8 convert_reduce_fusion
  586.9 2.0 fusion.2
  588.8 0.0 copy-done.5
  588.8 0.0 copy-done
  588.8 1.0 fusion.13
  589.9 0.4 fusion.40
  590.2 0.2 fusion.16
  590.4 0.0 copy-start.1
  590.4 0.4 convolution_convert_fusion
  590.8 0.1 copy.21
  590.9 40.3 %all_to_all.13 = bf16[8,64,192]{2,1,0:T(8,128)(2,1)S(1)} all-to-all(bf16[8,64,192]{2,1,0:T(8,128)(2,1)S(1)} %bitcast.31), channel_id=1, replica_groups=mesh['dp'=64,'seq'=8] {'seq'}, dimensions={0} | all-to-all | bytes 393216 | tf_op jit(solution)/shard_map/all_to_all | solution.py:76
  631.2 0.3 copy.22
  631.6 0.2 reshape.62
  631.7 0.0 copy-done.1
  631.7 0.7 fusion.24
  (4 shorter events, 0.1 us)
Async XLA Ops:
  6.5 342.6 %all-gather.3.cloned.1.call-start = ((), (), s32[]{:S(2)}) async-start(), calls=%async_computation.1 | async-start | bytes 19169280 | tf_op jit(solution)/shard_map/all_gather | solution.py:61
  41.8 3.0 copy-start.2
  44.8 540.3 %all-gather.5.cloned.1.call-start = ((), (), s32[]{:S(2)}) async-start(), calls=%async_computation.2 | async-start | bytes 1769472 | tf_op jit(solution)/shard_map/all_gather | solution.py:63
  44.8 341.0 %collective-permute-start = (bf16[2,768]{1,0:T(2,128)(2,1)S(1)}, bf16[2,768]{1,0:T(2,128)(2,1)S(1)}, u32[]{:S(2)}, u32[]{:S(2)}) collective-permute-start(bf16[2,768]{1,0:T(2,128)(2,1)S(1)} %get-tuple-element.25), channel_id=1, source_target_pairs={{0,1},{1,2},{2,3},{3,4},{4,5},{5,6},{6,7},{8,9},{9,10},{10,11},{11... | collective-permute-start | bytes 9224 | tf_op jit(solution)/shard_map/ppermute | solution.py:15
  48.4 337.9 %collective-permute-start.1 = (bf16[2,768]{1,0:T(2,128)(2,1)S(1)}, bf16[2,768]{1,0:T(2,128)(2,1)S(1)}, u32[]{:S(2)}, u32[]{:S(2)}) collective-permute-start(bf16[2,768]{1,0:T(2,128)(2,1)S(1)} %get-tuple-element.26), channel_id=1, source_target_pairs={{1,0},{2,1},{3,2},{4,3},{5,4},{6,5},{7,6},{9,8},{10,9},{11,10},{12... | collective-permute-start | bytes 9224 | tf_op jit(solution)/shard_map/ppermute | solution.py:18
  386.9 0.7 copy-start.4
  387.6 2.6 copy-start.3
  388.3 200.5 %copy-start.5 = (f32[1536]{0:T(1024)S(1)}, f32[1536]{0:T(1024)}, u32[]{:S(2)}) copy-start(f32[1536]{0:T(1024)} %param.8) | copy-start | bytes 18436
  585.0 3.8 copy-start
  590.4 41.3 %copy-start.1 = (bf16[64,1536]{1,0:T(8,128)(2,1)S(1)}, bf16[64,1536]{1,0:T(8,128)(2,1)}, u32[]{:S(2)}) copy-start(bf16[64,1536]{1,0:T(8,128)(2,1)} %reduce_max.19) | copy-start | bytes 589828
Sparse Core Ops, SparseCore 0:
  44.9 304.1 all-gather.2
  390.3 32.9 all-gather.4
where the time goes:
time: 640 us; the launch traced here: 639 us
  waiting for transfers between devices  299 us (47%)
  blocking collectives  269 us (42%)
  local copies, waits for them, and re-layouts  41.1 us (6%)
  between operations  13.6 us (2%)
  other arithmetic  6.45 us (1%)
    all_gather x1, waiting for transfers between devices, shards(): lax.all_gather(columns, 'dp', axis=1, tiled=True)  299 us
    all_gather x1, blocking collectives, shards(): lax.all_gather(qkv_weight, 'dp', axis=0, tiled=True)  195 us
    all_to_all x1, blocking collectives, shards(): lax.all_to_all(outputs, 'seq', split_axis=0, concat_axis=1, tiled=True)  40.3 us
    slice x1, local copies, waits for them, and re-layouts, conv_piece(): piece[tap]  36.2 us
    all_gather x1, blocking collectives, shards(): columns = lax.all_gather(conv_weight, 'seq', axis=2, tiled=True)  34.2 us
  transfers between devices with their start and end apart: 4, of which 1 were waited for; matrix products, arithmetic and copies ran while one was open for 6% of the time, Pallas kernels for 0%

commit v1 on v0

v1 whole, which is shorter than its diff:
```python
import jax
import jax.numpy as jnp
from jax import lax
from jax.sharding import PartitionSpec as P

HK = 64
HV = 192


def attend(query, keys, values):
    scale = query.shape[1] ** (-0.5)
    scores = jnp.dot(query, keys.T, preferred_element_type=jnp.float32) * scale
    top = jnp.max(scores, axis=-1, keepdims=True)
    expo = jnp.exp(scores - top)
    probs = (expo / jnp.sum(expo, axis=-1, keepdims=True)).astype(jnp.bfloat16)
    return jnp.dot(probs, values, preferred_element_type=jnp.float32).astype(jnp.bfloat16)


def shards(features, conv_weight, conv_bias, norm_gain, qkv_weight):
    taps, _, cols = conv_weight.shape
    half = taps // 2
    weight = lax.all_gather(conv_weight, "dp", axis=1, tiled=True)
    seq_in = lax.all_gather(features[0], "seq", axis=0, tiled=True)
    projection = lax.all_gather(qkv_weight, "dp", axis=0, tiled=True)
    rows = seq_in.shape[0]
    padded = jnp.pad(seq_in, ((half, half), (0, 0)))
    total = jnp.zeros((rows, cols), jnp.float32)
    for tap in range(taps):
        total = total + jnp.dot(padded[tap : tap + rows], weight[tap], preferred_element_type=jnp.float32)
    mine = lax.axis_index("seq") * cols
    total = total + lax.dynamic_slice_in_dim(conv_bias, mine, cols)
    active = jax.nn.gelu(total, approximate=True)
    pooled = jnp.max(active.reshape(rows // 2, 2, cols), axis=1).astype(jnp.bfloat16)
    whole = lax.all_gather(pooled, "seq", axis=1, tiled=True)
    values32 = whole.astype(jnp.float32)
    mean = jnp.mean(values32, axis=-1, keepdims=True)
    centred = values32 - mean
    var = jnp.mean(centred * centred, axis=-1, keepdims=True)
    normed = (centred / jnp.sqrt(var + 1e-05) * norm_gain).astype(jnp.bfloat16)
    qkv = jnp.dot(normed, projection, preferred_element_type=jnp.float32).astype(jnp.bfloat16)
    width = 2 * HK + HV
    outputs = attend(qkv[:, 0:HK], qkv[:, HK : 2 * HK], qkv[:, 2 * HK : width])
    mixed = (pooled.astype(jnp.float32) + outputs.astype(jnp.float32)).astype(jnp.bfloat16)
    arrived = lax.all_to_all(mixed, "seq", split_axis=0, concat_axis=1, tiled=True)
    return arrived[None]


def solution(mesh):
    return jax.shard_map(
        shards,
        mesh=mesh,
        in_specs=(P("dp", "seq", None), P(None, "dp", "seq"), P(), P(), P("dp", "seq")),
        out_specs=P("dp", "seq", None),
        check_vma=False,
    )
```

time: 640 us -> 464 us (0.72)
  waiting for transfers between devices: 299 us -> 172 us
  blocking collectives: 269 us -> 242 us
  local copies, waits for them, and re-layouts: 41.1 us -> 22.6 us
    all_gather x2 -> x3, waiting for transfers between devices: 299 us -> 171 us  [the longest x1 147 us: shards(): weight = lax.all_gather(conv_weight, 'dp', axis=1, tiled=True)]
    all_gather x2 -> x1, blocking collectives: 229 us -> 201 us  [shards(): projection = lax.all_gather(qkv_weight, 'dp', axis=0, tiled=True)]
    slice x2 -> x1, local copies, waits for them, and re-layouts: 36.2 us -> 11.1 us  [shards(): weight[tap]]
    unnamed x13 -> x22, local copies, waits for them, and re-layouts: 1.22 us -> 8.22 us
  transfers between devices with their start and end apart: 4 -> 3, of which waited for: 1 -> 2; matrix products, arithmetic and copies ran while one was open for 6% -> 4% of each run, Pallas kernels for 0% -> 0%
where the time goes in v1:
time: 464 us
  blocking collectives  242 us (52%)
  waiting for transfers between devices  172 us (37%)
  local copies, waits for them, and re-layouts  22.6 us (5%)
  between operations  13.3 us (3%)
  matrix products  9.86 us (2%)
    all_gather x1, blocking collectives, shards(): projection = lax.all_gather(qkv_weight, 'dp', axis=0, tiled=True)  201 us
    all_gather x1, waiting for transfers between devices, shards(): weight = lax.all_gather(conv_weight, 'dp', axis=1, tiled=True)  147 us
    all_to_all x1, blocking collectives, shards(): lax.all_to_all(mixed, 'seq', split_axis=0, concat_axis=1, tiled=True)  40.5 us
    all_gather x1, waiting for transfers between devices, shards(): seq_in = lax.all_gather(features[0], 'seq', axis=0, tiled=True)  24.3 us
    slice x1, local copies, waits for them, and re-layouts, shards(): weight[tap]  11.1 us
  transfers between devices with their start and end apart: 3, of which 2 were waited for; matrix products, arithmetic and copies ran while one was open for 4% of the time, Pallas kernels for 0%

profile of v1, /device:TPU:1, one launch (start us, length us, event | category | flops | bytes accessed | tf_op | source)
XLA Modules:
  0.0 463.6 jit_solution(3690636125033973222)
XLA Ops:
  6.5 0.0 all-gather.5.cloned.1.call-start
  6.5 1.4 copy.17
  7.9 0.0 all-gather.5.cloned.1.call-update
  8.0 0.0 all-gather.9.cloned.1.call-start
  8.0 0.7 all-gather.9.cloned.1.call-update
  8.7 0.0 all-gather.7.cloned.1.call-start
  8.8 0.8 dynamic_slice.3
  9.6 147.1 %all-gather.5.cloned.1.call-done = bf16[5,768,192]{2,0,1:T(8,128)(2,1)} async-done(((bf16[5,12,192]{2,0,1:T(8,128)(2,1)}), bf16[5,768,192]{2,0,1:T(8,128)(2,1)}) %all-gather.5.cloned.1.call-update) | async-done | bytes 1474576 | tf_op jit(solution)/shard_map/all_gather | solution.py:22
  156.7 11.1 %fusion.60 = (bf16[1,768,192]{2,0,1:T(2,128)(2,1)S(1)}, bf16[1,768,192]{2,0,1:T(2,128)(2,1)S(1)}, bf16[1,768,192]{2,0,1:T(2,128)(2,1)}, bf16[1,768,192]{2,0,1:T(2,128)(2,1)S(1)}, bf16[1,768,192]{2,0,1:T(2,128)(2,1)S(1)}) fusion(bf16[5,768,192]{2,0,1:T(8,128)(2,1)} %all-gather.5.cloned.1.call-done), kind=kLoop, calls=%fused_computation.57 | loop fusion | bytes 2949120 | tf_op jit(solution)/shard_map/slice | solution.py:29
  167.8 2.8 copy.28
  170.6 0.5 copy.27
  171.1 0.0 copy-start.3
  171.1 0.5 copy.29
  171.6 1.6 copy.31
  173.3 24.3 %all-gather.9.cloned.1.call-done = bf16[1,1024,768]{2,1,0:T(8,128)(2,1)} async-done(((bf16[1,128,768]{2,1,0:T(8,128)(2,1)}), bf16[1,1024,768]{2,1,0:T(8,128)(2,1)}) %all-gather.9.cloned.1.call-update) | async-done | bytes 1572880 | tf_op jit(solution)/shard_map/all_gather | solution.py:23
  197.5 0.0 copy-done.3
  197.5 3.1 fusion.9
  200.6 0.0 copy-done.1
  200.7 0.0 copy-done.4
  200.7 1.6 fusion.5
  202.2 0.5 copy.30
  202.7 1.8 fusion.15
  204.5 0.0 copy-start.7
  204.5 0.7 convolution_add_fusion
  205.2 0.5 copy-done.7
  205.7 0.9 fusion.44
  206.6 0.0 copy-start.5
  206.6 0.2 copy.23
  206.8 0.3 reshape.23
  207.1 1.5 reduce_max.18
  208.6 0.8 copy.24
  209.4 0.0 all-gather.7.cloned.1.call-update
  209.4 0.0 copy-done.5
  209.4 201.3 %all_gather.15 = bf16[1536,320]{1,0:T(8,128)(2,1)S(1)} all-gather(bf16[24,320]{1,0:T(8,128)(2,1)S(1)} %copy-done.5), channel_id=1, replica_groups=mesh['dp'=64,'seq'=8] {'dp'}, dimensions={0}, use_global_device_ids=true | all-gather | bytes 998400 | tf_op jit(solution)/shard_map/all_gather | solution.py:24
  410.7 1.8 convert_reduce_fusion
  412.5 0.1 copy-done
  412.6 0.5 fusion.2
  413.1 0.0 copy-done.6
  413.1 1.0 fusion.27
  414.1 0.0 copy-start.2
  414.1 0.4 fusion.61
  414.5 0.2 fusion.37
  414.7 0.4 copy-done.2
  415.0 0.4 fusion.32
  415.4 0.1 copy.25
  415.5 40.5 %all_to_all.16 = bf16[8,64,192]{2,1,0:T(8,128)(2,1)S(1)} all-to-all(bf16[8,64,192]{2,1,0:T(8,128)(2,1)S(1)} %bitcast.25), channel_id=1, replica_groups=mesh['dp'=64,'seq'=8] {'seq'}, dimensions={0} | all-to-all | bytes 393216 | tf_op jit(solution)/shard_map/all_to_all | solution.py:44
  456.0 0.1 copy.26
  456.2 0.9 broadcast_in_dim.2
  (7 shorter events, 0.0 us)
Async XLA Ops:
  6.5 150.1 %all-gather.5.cloned.1.call-start = ((), (), s32[]{:S(2)}) async-start(), calls=%async_computation.1 | async-start | bytes 3194880 | tf_op jit(solution)/shard_map/all_gather | solution.py:22
  8.0 189.6 %all-gather.9.cloned.1.call-start = ((), (), s32[]{:S(2)}) async-start(), calls=%async_computation.3 | async-start | bytes 1769472 | tf_op jit(solution)/shard_map/all_gather | solution.py:23
  8.7 402.0 %all-gather.7.cloned.1.call-start = ((), (), s32[]{:S(2)}) async-start(), calls=%async_computation.2 | async-start | bytes 1769472 | tf_op jit(solution)/shard_map/all_gather | solution.py:34
  171.1 26.4 %copy-start.3 = (bf16[1,768,192]{1,2,0:T(8,128)(2,1)S(1)}, bf16[1,768,192]{1,2,0:T(8,128)(2,1)}, u32[]{:S(2)}) copy-start(bf16[1,768,192]{1,2,0:T(8,128)(2,1)} %copy.28) | copy-start | bytes 884740
  197.5 3.1 copy-start.1
  197.5 3.1 copy-start.4
  204.5 1.1 copy-start.7
  206.6 2.8 copy-start.5
  410.7 1.9 copy-start
  410.7 2.4 copy-start.6
  414.1 0.9 copy-start.2
Sparse Core Ops, SparseCore 0:
  11.9 144.7 all-gather.4
  158.7 38.7 all-gather.8
  209.5 40.7 all-gather.6

commit v2 on v1

v2 whole, which is shorter than its diff:
```python
import functools

import jax
import jax.numpy as jnp
from jax import lax
from jax.experimental import pallas as pl
from jax.experimental.pallas import tpu as pltpu
from jax.sharding import PartitionSpec as P

HK = 64
HV = 192
NH = 2
NX = 4
BF = jnp.bfloat16
F32 = jnp.float32


def kernel(
    nz, nx, ny,
    feat_ref, conv_ref, bias_ref, gain_ref, proj_ref, out_ref,
    feat, edge, edges, ext, prev, later,
    w0, w1, wbuild, wc, p0, p1, pbuild, pw,
    pool, qkv, mixed, landed,
    send_sems, r_feat, r_edge, r_w0, r_p0, r_w1, r_p1,
    r_wup, r_wdown, r_wsib, r_pup, r_pdown, r_psib, r_pool, r_kv, r_mix,
):
    dp, seq = lax.axis_index("dp"), lax.axis_index("seq")
    h, z, x = lax.div(dp, nz * nx), lax.rem(lax.div(dp, nx), nz), lax.rem(dp, nx)
    y, c = lax.div(seq, 2), lax.rem(seq, 2)

    def at(hh, zz, xx, yy, cc):
        return ((hh * nz + zz) * nx + xx, yy * 2 + cc)

    sibling = at(h, z, x, y, 1 - c)
    above = at(h, lax.rem(z + 1, nz), x, y, c)
    below = at(h, lax.rem(z + nz - 1, nz), x, y, c)
    others_y = [lax.rem(y + d, ny) for d in range(1, ny)]
    others_x = [lax.rem(x + d, nx) for d in range(1, nx)]

    partners = [sibling, above, below, at(1 - h, z, x, y, 0), at(1 - h, z, x, y, 1)]
    partners += [at(h, z, x, yy, c) for yy in others_y]
    partners += [at(h, z, x, yy, 1 - c) for yy in others_y]
    partners += [at(h, z, xx, y, c) for xx in others_x]
    barrier = pltpu.get_barrier_semaphore()
    for device in partners:
        pl.semaphore_signal(barrier, inc=1, device_id=device, device_id_type=pl.DeviceIdType.MESH)
    pl.semaphore_wait(barrier, len(partners))

    pending = []

    def copy(src, dst, recv, device, index):
        return pltpu.make_async_remote_copy(
            src_ref=src, dst_ref=dst, send_sem=send_sems.at[index], recv_sem=recv,
            device_id=device, device_id_type=pl.DeviceIdType.MESH,
        )

    def send(src, dst, recv, device):
        cp = copy(src, dst, recv, device, len(pending))
        cp.start()
        pending.append(cp)

    def arrived(dst, recv):
        copy(dst, dst, recv, sibling, 0).wait_recv()

    rows = conv_ref.shape[1]
    send(conv_ref, w0.at[c], r_w0.at[c], at(1 - h, z, x, y, h))
    send(proj_ref, p0.at[c], r_p0.at[c], at(1 - h, z, x, y, h))
    extra = [
        copy(conv_ref, w0.at[c], r_w0.at[c], sibling, len(pending)),
        copy(proj_ref, p0.at[c], r_p0.at[c], sibling, len(pending) + 1),
    ]
    own = c == h

    @pl.when(jnp.logical_not(own))
    def _():
        for cp in extra:
            cp.start()

    used = len(pending) + 2
    pending.extend([None, None])

    @pl.when(own)
    def _():
        w0[c] = conv_ref[...]
        p0[c] = proj_ref[...]

    half_rows = feat_ref.shape[0]
    first = feat_ref[0:16, :].astype(F32)[0:1]
    last = feat_ref[half_rows - 16 : half_rows, :].astype(F32)[15:16]
    edge[...] = jnp.concatenate([first, last], axis=0).astype(BF)
    feat[y] = feat_ref[...]
    for yy in others_y:
        send(edge, edges.at[1 + y], r_edge.at[y], at(h, z, x, yy, 1 - c))
    send(edge, edges.at[1 + y], r_edge.at[y], sibling)
    for yy in others_y:
        send(feat_ref, feat.at[y], r_feat.at[y], at(h, z, x, yy, c))
    zero = jnp.zeros(edge.shape, BF)
    edges[0] = zero
    edges[ny + 1] = zero

    arrived(w0.at[1 - c], r_w0.at[1 - c])

    @pl.when(jnp.logical_not(own))
    def _():
        arrived(w0.at[c], r_w0.at[c])

    w1[x] = jnp.concatenate([w0[0].astype(F32), w0[1].astype(F32)], axis=2).astype(BF)
    for xx in others_x:
        send(w1.at[x], w1.at[x], r_w1.at[x], at(h, z, xx, y, c))

    arrived(p0.at[1 - c], r_p0.at[1 - c])

    @pl.when(jnp.logical_not(own))
    def _():
        arrived(p0.at[c], r_p0.at[c])

    a, b = p0[0].astype(F32), p0[1].astype(F32)
    p1[x] = jnp.concatenate(
        [a[:, :HK], b[:, :HK], a[:, HK : 2 * HK], b[:, HK : 2 * HK], a[:, 2 * HK :], b[:, 2 * HK :]],
        axis=1,
    ).astype(BF)
    for xx in others_x:
        send(p1.at[x], p1.at[x], r_p1.at[x], at(h, z, xx, y, c))

    taps = conv_ref.shape[0]
    w_rows = rows * nx
    p_rows = proj_ref.shape[0] * nx

    def w_block(cc, zz):
        return wc.at[:, pl.ds(pl.multiple_of((cc * nz + zz) * w_rows, 16), w_rows), :]

    def p_block(cc, zz):
        return pw.at[pl.ds(pl.multiple_of((cc * nz + zz) * p_rows, 16), p_rows), :]

    ups, downs = nz // 2, nz - 1 - nz // 2

    def ring(block, r_up, r_down, r_sib):
        mine = block(c, z)
        send(mine, mine, r_up.at[0], above)
        if downs:
            send(mine, mine, r_down.at[0], below)
        send(mine, mine, r_sib.at[0], sibling)
        for d in range(ups):
            got = block(c, lax.rem(z - 1 - d + nz, nz))
            arrived(got, r_up.at[d])
            if d + 1 < ups:
                send(got, got, r_up.at[d + 1], above)
            send(got, got, r_sib.at[1 + d], sibling)
            if d < downs:
                got = block(c, lax.rem(z + 1 + d, nz))
                arrived(got, r_down.at[d])
                if d + 1 < downs:
                    send(got, got, r_down.at[d + 1], below)
                send(got, got, r_sib.at[1 + ups + d], sibling)
            yield d

    def from_sibling(block, r_sib):
        zs = [z] + [lax.rem(z - 1 - d + nz, nz) for d in range(ups)] + [lax.rem(z + 1 + d, nz) for d in range(downs)]
        for k, zz in enumerate(zs):
            arrived(block(1 - c, zz), r_sib.at[k])

    for xx in others_x:
        arrived(w1.at[xx], r_w1.at[xx])
    for t in range(taps):
        for xx in range(nx):
            wbuild[t, rows * xx : rows * (xx + 1), :] = w1[xx, t].astype(F32)
    w_mine = pl.multiple_of((c * nz + z) * w_rows, 16)
    for t in range(taps):
        wc[t, pl.ds(w_mine, w_rows), :] = wbuild[t].astype(BF)

    def shifted(yy):
        ext[8 : 8 + half_rows, :] = feat[yy].astype(F32)
        before = edges[yy + c].astype(F32)
        after = edges[yy + c + 1].astype(F32)
        ext[7:8, :] = before[1:2]
        ext[8 + half_rows : 9 + half_rows, :] = after[0:1]
        prev[yy] = ext[7 : 7 + half_rows, :].astype(BF)
        later[yy] = ext[9 : 9 + half_rows, :].astype(BF)

    conv_ring = ring(w_block, r_wup, r_wdown, r_wsib)
    done = 0
    for d in conv_ring:
        if d == 0:
            for xx in others_x:
                arrived(p1.at[xx], r_p1.at[xx])
            step = proj_ref.shape[0]
            for xx in range(nx):
                pbuild[step * xx : step * (xx + 1), :] = p1[xx].astype(F32)
            pw[pl.ds(pl.multiple_of((c * nz + z) * p_rows, 16), p_rows), :] = pbuild[...].astype(BF)
        if d == ups - 1:
            for yy in others_y:
                arrived(edges.at[1 + yy], r_edge.at[yy])
            arrived(edges.at[1 + y], r_edge.at[y])
            for yy in others_y:
                arrived(feat.at[yy], r_feat.at[yy])
            for yy in range(ny):
                shifted(yy)
    from_sibling(w_block, r_wsib)

    cin = wc.shape[1]
    cols = wc.shape[2]
    bias = bias_ref[:, pl.ds(pl.multiple_of(y * cols, 128), cols)]
    wflat = wc.reshape(taps * cin, cols)

    def dot(left, right):
        return jnp.dot(left, right, preferred_element_type=F32)

    def gelu(value):
        value = value + bias
        inner = 0.7978845608028654 * (value + 0.044715 * (value * value * value))
        return value * (0.5 * (1.0 + jnp.tanh(inner)))

    for yy in range(ny):
        before, now, after = prev[yy], feat[yy], later[yy]
        even = dot(before, wflat[0 : 2 * cin, :]) + dot(now, wflat[2 * cin : 4 * cin, :])
        even = even + dot(after[:, :cin], wflat[4 * cin :, :])
        odd = dot(before[:, cin:], wflat[0:cin, :]) + dot(now, wflat[cin : 3 * cin, :])
        odd = odd + dot(after, wflat[3 * cin :, :])
        pool[y, yy * half_rows : (yy + 1) * half_rows, :] = jnp.maximum(gelu(even), gelu(odd)).astype(BF)
    for yy in others_y:
        send(pool.at[y], pool.at[y], r_pool.at[y], at(h, z, x, yy, c))

    for _ in ring(p_block, r_pup, r_pdown, r_psib):
        pass
    from_sibling(p_block, r_psib)

    for yy in others_y:
        arrived(pool.at[yy], r_pool.at[yy])
    width = ny * cols
    total = functools.reduce(
        jnp.add, [jnp.sum(pool[yy].astype(F32), axis=1, keepdims=True) for yy in range(ny)]
    )
    mean = total * (1.0 / width)
    square = functools.reduce(
        jnp.add, [jnp.sum(jnp.square(pool[yy].astype(F32) - mean), axis=1, keepdims=True) for yy in range(ny)]
    )
    inverse = 1.0 / jnp.sqrt(square * (1.0 / width) + 1e-05)
    acc = None
    for yy in range(ny):
        normed = ((pool[yy].astype(F32) - mean) * inverse * gain_ref[:, yy * cols : (yy + 1) * cols]).astype(BF)
        part = dot(normed, pw[yy * cols : (yy + 1) * cols, :])
        acc = part if acc is None else acc + part
    qkv[c] = acc.astype(BF)
    send(qkv.at[c], qkv.at[c], r_kv.at[c], sibling)
    arrived(qkv.at[1 - c], r_kv.at[1 - c])

    query = qkv[c, :, : 2 * HK]
    lane = lax.broadcasted_iota(jnp.int32, query.shape, 1)
    outs = []
    for head in range(2):
        q = jnp.where((lane < HK) if head == 0 else (lane >= HK), query, jnp.zeros_like(query))
        scores = [
            lax.dot_general(q, qkv[k, :, 2 * HK : 4 * HK], (((1,), (1,)), ((), ())), preferred_element_type=F32)
            * (HK ** -0.5)
            for k in range(2)
        ]
        top = jnp.maximum(*[jnp.max(s, axis=1, keepdims=True) for s in scores])
        expo = [jnp.exp(s - top) for s in scores]
        inv = 1.0 / (jnp.sum(expo[0], axis=1, keepdims=True) + jnp.sum(expo[1], axis=1, keepdims=True))
        probs = [(e * inv).astype(BF) for e in expo]
        outs.append(dot(probs[0], qkv[0, :, 4 * HK :]) + dot(probs[1], qkv[1, :, 4 * HK :]))
    lane = lax.broadcasted_iota(jnp.int32, outs[0].shape, 1)
    attended = jnp.where(lane < HV, outs[0], outs[1]).astype(BF)
    mixed[...] = (pool[y].astype(F32) + attended.astype(F32)).astype(BF).reshape(mixed.shape)

    for yy in others_y:
        send(mixed.at[yy], landed.at[y], r_mix.at[y], at(h, z, x, yy, c))
    landed[y] = mixed[y]
    for yy in others_y:
        arrived(landed.at[yy], r_mix.at[yy])
    for yy in range(ny):
        out_ref[:, yy * cols : (yy + 1) * cols] = landed[yy]

    for cp in pending:
        if cp is not None:
            cp.wait_send()

    @pl.when(jnp.logical_not(own))
    def _():
        for cp in extra:
            cp.wait_send()


def shards(features, conv_weight, conv_bias, norm_gain, qkv_weight):
    dp, ny = lax.axis_size("dp"), lax.axis_size("seq") // 2
    nx, nz = NX, dp // (NH * NX)
    taps, rows, cols = conv_weight.shape
    cols, cin, width = 2 * cols, rows * dp, 2 * ny * cols
    half_rows = features.shape[1] // 2
    step, heads = qkv_weight.shape
    heads = 2 * heads
    positions = half_rows * ny
    dma = pltpu.SemaphoreType.DMA
    vmem = pltpu.VMEM
    ups, downs = nz // 2, nz - 1 - nz // 2
    sends = 4 + ny + (ny - 1) + 2 * (nx - 1) + 2 * (2 * nz - 1) + (ny - 1) + 1 + (ny - 1)
    scratch = [
        vmem((ny, half_rows, 2 * cin), BF),
        vmem((2, 2 * cin), BF),
        vmem((ny + 2, 2, 2 * cin), BF),
        vmem((half_rows + 16, 2 * cin), F32),
        vmem((ny, half_rows, 2 * cin), BF),
        vmem((ny, half_rows, 2 * cin), BF),
        vmem((2,) + conv_weight.shape, BF),
        vmem((nx, taps, rows, cols), BF),
        vmem((taps, nx * rows, cols), F32),
        vmem((taps, cin, cols), BF),
        vmem((2,) + qkv_weight.shape, BF),
        vmem((nx, step, heads), BF),
        vmem((nx * step, heads), F32),
        vmem((width, heads), BF),
        vmem((ny, positions, cols), BF),
        vmem((2, positions, heads), BF),
        vmem((ny, half_rows, cols), BF),
        vmem((ny, half_rows, cols), BF),
        dma((sends,)), dma((ny,)), dma((ny,)), dma((2,)), dma((2,)), dma((nx,)), dma((nx,)),
        dma((ups,)), dma((max(downs, 1),)), dma((nz,)),
        dma((ups,)), dma((max(downs, 1),)), dma((nz,)),
        dma((ny,)), dma((2,)), dma((ny,)),
    ]
    out = pl.pallas_call(
        functools.partial(kernel, nz, nx, ny),
        out_shape=jax.ShapeDtypeStruct((half_rows, width), BF),
        in_specs=[pl.BlockSpec(memory_space=pltpu.VMEM)] * 5,
        out_specs=pl.BlockSpec(memory_space=pltpu.VMEM),
        scratch_shapes=scratch,
        compiler_params=pltpu.CompilerParams(
            collective_id=0, has_side_effects=True, vmem_limit_bytes=48 * 2**20
        ),
        name="section",
    )(
        features[0].reshape(half_rows, 2 * cin),
        conv_weight,
        conv_bias.reshape(1, width),
        norm_gain.reshape(1, width),
        qkv_weight,
    )
    return out[None]


def solution(mesh):
    return jax.shard_map(
        shards,
        mesh=mesh,
        in_specs=(P("dp", "seq", None), P(None, "dp", "seq"), P(), P(), P("dp", "seq")),
        out_specs=P("dp", "seq", None),
        check_vma=False,
    )
```

time: 464 us -> 81.6 us (0.18)
  blocking collectives: 242 us -> 0 us
  waiting for transfers between devices: 172 us -> 0 us
  Pallas kernels: 0 us -> 78.1 us
  local copies, waits for them, and re-layouts: 22.6 us -> 2.42 us
  between operations: 13.3 us -> 0.05 us
  matrix products: 9.86 us -> 0 us
    all_gather x1 -> x0, blocking collectives: 201 us -> none  [shards(): projection = lax.all_gather(qkv_weight, 'dp', axis=0, tiled=True)]
    all_gather x3 -> x0, waiting for transfers between devices: 171 us -> none  [the longest x1 147 us: shards(): weight = lax.all_gather(conv_weight, 'dp', axis=1, tiled=True)]
    pallas_call x0 -> x1, Pallas kernels: none -> 78.1 us  [shards(): pl.pallas_call(functools.partial(kernel, nz, nx, ny), out_shape=jax.Shape...]
    all_to_all x1 -> x0, blocking collectives: 40.5 us -> none  [shards(): lax.all_to_all(mixed, 'seq', split_axis=0, concat_axis=1, tiled=True)]
    slice x1 -> x0, local copies, waits for them, and re-layouts: 11.1 us -> none  [shards(): weight[tap]]
    dot_general x8 -> x0, matrix products: 9.86 us -> none  [the longest x5 8.1 us: shards(): jnp.dot(padded[tap:tap + rows], weight[tap], preferred_element_type=jnp.f...]
    unnamed x22 -> x7, local copies, waits for them, and re-layouts: 8.22 us -> 0.7 us
  transfers between devices with their start and end apart: 3 -> 0, of which waited for: 2 -> 0; matrix products, arithmetic and copies ran while one was open for 4% -> 0% of each run, Pallas kernels for 0% -> 0%
where the time goes in v2:
time: 81.6 us; the launch traced here: 80.6 us
  Pallas kernels  78.1 us (96%)
  local copies, waits for them, and re-layouts  2.42 us (3%)
    pallas_call x1, Pallas kernels, shards(): pl.pallas_call(functools.partial(kernel, nz, nx, ny), out_shape=jax.Shape...  78.1 us

profile of v2, /device:TPU:1, one launch (start us, length us, event | category | flops | bytes accessed | tf_op | source)
XLA Modules:
  0.0 80.6 jit_solution(12552115928301070127)
XLA Ops:
  0.0 0.0 copy-start.2
  0.0 0.7 reshape.6.bias_ref
  0.7 0.0 copy-done.2
  0.7 0.0 copy-start
  0.7 0.0 copy-start.1
  0.8 1.0 %reshape_squeeze.3.feat_ref = bf16[64,1536]{1,0:T(8,128)(2,1)S(1)} reshape(bf16[1,128,768]{2,1,0:T(8,128)(2,1)} %param.5) | data formatting | bytes 393216 | tf_op jit(solution)/shard_map/reshape;squeeze | solution.py:332
  1.8 0.0 copy-done
  1.8 0.0 copy-done.1
  1.8 78.1 %section.1 = bf16[64,1536]{1,0:T(8,128)(2,1)S(1)} custom-call(bf16[64,1536]{1,0:T(8,128)(2,1)S(1)} %reshape_squeeze.3.feat_ref, bf16[5,12,192]{2,1,0:T(8,128)(2,1)S(1)} %copy-done, f32[1,1536]{1,0:T(1,128)S(1)} %reshape.6.bias_ref, f32[1,1536]{1,0:T(1,128)S(1)} %reshape.7.gain_ref, bf16[24,320]{1,0:T(8,128)(2,1)S(1)} %copy-done.1), custom_call_target="tpu_custom_call" | custom-call | tf_op jit(solution)/shard_map/section/pallas_call | solution.py:321
  79.9 0.7 copy.7
  (1 shorter events, 0.0 us)
Async XLA Ops:
  0.0 0.7 copy-start.2
  0.7 1.0 %copy-start = (bf16[5,12,192]{2,1,0:T(8,128)(2,1)S(1)}, bf16[5,12,192]{2,1,0:T(8,128)(2,1)}, u32[]{:S(2)}) copy-start(bf16[5,12,192]{2,1,0:T(8,128)(2,1)} %conv_ref.1) | copy-start | bytes 69124
  0.7 1.0 %copy-start.1 = (bf16[24,320]{1,0:T(8,128)(2,1)S(1)}, bf16[24,320]{1,0:T(8,128)(2,1)}, u32[]{:S(2)}) copy-start(bf16[24,320]{1,0:T(8,128)(2,1)} %proj_ref.1) | copy-start | bytes 46084

commit v3 on v1

v3 whole, which is shorter than its diff:
```python
import functools

import jax
import jax.numpy as jnp
from jax import lax
from jax.experimental import pallas as pl
from jax.experimental.pallas import tpu as pltpu
from jax.sharding import PartitionSpec as P

HK = 64
HV = 192
NH = 2
NX = 4
BF = jnp.bfloat16
F32 = jnp.float32
P_START = 3
PARTS = ((0, 2), (2, 2), (4, 1))


def kernel(
    nz, nx, ny,
    feat_in, conv_in, bias_in, gain_in, proj_in, out_ref,
    feat_ref, conv_ref, bias_ref, gain_ref, proj_ref,
    mine, feat, edge, edges, ext, wide, prev, later,
    wpack, wown, w0, w1, wflat32, wbuild, wc, pown, p0, p1, pbuild, pw,
    pool, qkv, mixed, landed,
    in_sems, send_sems, r_feat, r_edge, r_w0, r_p0, r_w1, r_p1,
    r_wa, r_wb, r_wsib, r_pup, r_pdown, r_psib, r_pool, r_kv, r_mix,
):
    dp, seq = lax.axis_index("dp"), lax.axis_index("seq")
    h, z, x = lax.div(dp, nz * nx), lax.rem(lax.div(dp, nx), nz), lax.rem(dp, nx)
    y, c = lax.div(seq, 2), lax.rem(seq, 2)
    turn = 1 - 2 * c

    def at(hh, zz, xx, yy, cc):
        return ((hh * nz + zz) * nx + xx, yy * 2 + cc)

    def round_z(offset):
        return lax.rem(z + offset + 2 * nz, nz)

    def round_x(offset):
        return lax.rem(x + offset + nx, nx)

    sibling = at(h, z, x, y, 1 - c)
    z_next, z_last = at(h, round_z(turn), x, y, c), at(h, round_z(-turn), x, y, c)
    x_next, x_last = at(h, z, round_x(turn), y, c), at(h, z, round_x(-turn), y, c)
    others_y = [lax.rem(y + d, ny) for d in (2, 1, 3)]
    others_x = [lax.rem(x + d, nx) for d in range(1, nx)]

    partners = [sibling, z_next, z_last, at(1 - h, z, x, y, 0), at(1 - h, z, x, y, 1)]
    partners += [at(h, z, x, yy, c) for yy in others_y]
    partners += [at(h, z, x, yy, 1 - c) for yy in others_y]
    partners += [at(h, z, xx, y, c) for xx in others_x]
    inputs = ((conv_in, conv_ref), (feat_in, feat_ref), (proj_in, proj_ref), (bias_in, bias_ref), (gain_in, gain_ref))
    loads = [pltpu.make_async_copy(src, dst, in_sems.at[i]) for i, (src, dst) in enumerate(inputs)]
    for load in loads:
        load.start()
    barrier = pltpu.get_barrier_semaphore()
    for device in partners:
        pl.semaphore_signal(barrier, inc=1, device_id=device, device_id_type=pl.DeviceIdType.MESH)

    for load in loads:
        load.wait()

    half_rows, lanes = mine.shape
    cin = lanes // 2
    for k in range(cin // 128):
        ext[k] = feat_ref[:, 128 * k : 128 * (k + 1)].astype(F32)
        mine[:, 128 * k : 128 * (k + 1)] = ext[k, pl.ds(0, half_rows, stride=2), :].astype(BF)
        mine[:, cin + 128 * k : cin + 128 * (k + 1)] = ext[k, pl.ds(1, half_rows, stride=2), :].astype(BF)
    first = mine[0:16, :].astype(F32)[0:1]
    last = mine[half_rows - 16 :, :].astype(F32)[15:16]
    strips = [row[:, 128 * k : 128 * (k + 1)] for row in (first, last) for k in range(lanes // 128)]
    spare = edge.shape[0] - len(strips)
    edge[...] = jnp.concatenate(strips + [jnp.zeros((spare, 128), F32)], axis=0).astype(BF)
    zero = jnp.zeros(edge.shape, BF)
    edges[0] = zero
    edges[ny + 1] = zero
    own = c == h
    taps, rows, cols = conv_ref.shape
    p_in, p_cols = proj_ref.shape
    wpack[...] = jnp.zeros(wpack.shape, F32)
    for t in range(taps):
        wpack[rows * t : rows * (t + 1), :cols] = conv_ref[t].astype(F32)
    wown[...] = wpack[...].astype(BF)
    pown[...] = jnp.zeros(pown.shape, BF)
    pown[:p_in, :p_cols] = proj_ref[...]

    @pl.when(own)
    def _():
        w0[c] = wown[...]
        p0[c] = pown[...]

    pl.semaphore_wait(barrier, len(partners))

    pending = []

    def copy(src, dst, recv, device, index):
        return pltpu.make_async_remote_copy(
            src_ref=src, dst_ref=dst, send_sem=send_sems.at[index], recv_sem=recv,
            device_id=device, device_id_type=pl.DeviceIdType.MESH,
        )

    def send(src, dst, recv, device, when=None):
        cp = copy(src, dst, recv, device, len(pending))
        if when is None:
            cp.start()
        else:
            pl.when(when)(cp.start)
        pending.append((cp, when))

    def arrived(dst, recv):
        copy(dst, dst, recv, sibling, 0).wait_recv()

    middle = jnp.logical_or(y == 1, y == 2)
    pass_from, pass_to = jnp.where(y == 1, 3, 0), jnp.where(y == 1, 0, 3)

    def spread(ref, dst, recv):
        for yy in others_y:
            send(ref, dst, recv.at[y], at(h, z, x, yy, c), jnp.abs(yy - y) < 3)

    def pass_on(block, recv):
        @pl.when(middle)
        def _():
            arrived(block(pass_from), recv.at[pass_from])

        send(block(pass_from), block(pass_from), recv.at[pass_from], at(h, z, x, pass_to, c), middle)

    def rest(block, recv):
        for yy in others_y:
            @pl.when(jnp.logical_not(jnp.logical_and(middle, yy == pass_from)))
            def _():
                arrived(block(yy), recv.at[yy])

    other = jnp.logical_not(own)
    send(wown, w0.at[c], r_w0.at[c], at(1 - h, z, x, y, h))
    send(wown, w0.at[c], r_w0.at[c], sibling, other)

    feat[y] = mine[...]
    spread(mine, feat.at[y], r_feat)
    for yy in others_y:
        send(edge, edges.at[1 + y], r_edge.at[y], at(h, z, x, yy, 1 - c))
    send(edge, edges.at[1 + y], r_edge.at[y], sibling)
    send(pown, p0.at[c], r_p0.at[c], at(1 - h, z, x, y, h))
    send(pown, p0.at[c], r_p0.at[c], sibling, other)

    arrived(w0.at[1 - c], r_w0.at[1 - c])

    @pl.when(other)
    def _():
        arrived(w0.at[c], r_w0.at[c])

    w1[x] = jnp.concatenate([w0[0].astype(F32)[:, :cols], w0[1].astype(F32)[:, :cols]], axis=1).astype(BF)
    for xx in others_x:
        send(w1.at[x], w1.at[x], r_w1.at[x], at(h, z, xx, y, c))

    w_rows = rows * nx
    p_rows = p_in * nx
    ups, downs = nz // 2, nz - 1 - nz // 2
    count = len(PARTS)

    def carried(distance):
        return lax.rem(z + x + c + distance, 2) == 0

    def p_block(cc, zz):
        return pw.at[pl.ds(pl.multiple_of((cc * nz + zz) * p_rows, 16), p_rows), :]

    for xx in others_x:
        arrived(w1.at[xx], r_w1.at[xx])
    for xx in range(nx):
        wflat32[...] = w1[xx].astype(F32)
        for t in range(taps):
            wbuild[t, rows * xx : rows * (xx + 1), :] = wflat32[rows * t : rows * (t + 1), :]
    wc[c * nz + z] = wbuild[...].astype(BF)

    def w_block(j, cc, zz):
        tap, size = PARTS[j]
        return wc.at[cc * nz + zz, tap : tap + size]

    to_sibling = {}

    def w_start(j):
        block = w_block(j, c, z)
        send(block, block, r_wa.at[j, 0], z_next, carried(0))
        if downs:
            send(block, block, r_wb.at[j, 0], z_last, carried(0))
        send(block, block, r_wsib.at[j, 0], sibling)

    def ways(d):
        found = [(round_z(-turn * (1 + d)), r_wa, ups, z_next, x_next, 1 + d)]
        if d < downs:
            found.append((round_z(turn * (1 + d)), r_wb, downs, z_last, x_last, 1 + ups + d))
        return found

    def w_step(j, d):
        for zz, recv, steps, z_to, x_to, k in ways(d):
            block = w_block(j, c, zz)

            @pl.when(carried(1 + d))
            def _():
                arrived(block, recv.at[j, d])

            if d + 1 < steps:
                send(block, block, recv.at[j, d + 1], z_to, carried(1 + d))
            send(block, block, recv.at[j, d], x_to, carried(1 + d))
            cp = copy(block, block, r_wsib.at[j, k], sibling, len(pending))
            pl.when(carried(1 + d))(cp.start)
            pending.append((cp, None))
            to_sibling[j, k] = cp

    def w_finish(j, d):
        for zz, recv, steps, z_to, x_to, k in ways(d):
            @pl.when(carried(d))
            def _():
                arrived(w_block(j, c, zz), recv.at[j, d])
                to_sibling[j, k].start()

    def w_sibling(j):
        zs = [z] + [round_z(turn * (1 + d)) for d in range(ups)] + [round_z(-turn * (1 + d)) for d in range(downs)]
        for k, zz in enumerate(zs):
            arrived(w_block(j, 1 - c, zz), r_wsib.at[j, k])

    def p_join():
        arrived(p0.at[1 - c], r_p0.at[1 - c])

        @pl.when(other)
        def _():
            arrived(p0.at[c], r_p0.at[c])

        a, b = p0[0].astype(F32)[:, :p_cols], p0[1].astype(F32)[:, :p_cols]
        p1[x] = jnp.concatenate(
            [a[:, :HK], b[:, :HK], a[:, HK : 2 * HK], b[:, HK : 2 * HK], a[:, 2 * HK :], b[:, 2 * HK :]],
            axis=1,
        ).astype(BF)
        for xx in others_x:
            send(p1.at[x], p1.at[x], r_p1.at[x], at(h, z, xx, y, c))

    def p_start():
        for xx in others_x:
            arrived(p1.at[xx], r_p1.at[xx])
        for xx in range(nx):
            pbuild[p_in * xx : p_in * (xx + 1), :] = p1[xx].astype(F32)[:p_in]
        pw[pl.ds(pl.multiple_of((c * nz + z) * p_rows, 16), p_rows), :] = pbuild[...].astype(BF)
        block = p_block(c, z)
        send(block, block, r_pup.at[0], z_next)
        if downs:
            send(block, block, r_pdown.at[0], z_last)
        send(block, block, r_psib.at[0], sibling)

    def p_step(d):
        got = p_block(c, round_z(-turn * (1 + d)))
        arrived(got, r_pup.at[d])
        if d + 1 < ups:
            send(got, got, r_pup.at[d + 1], z_next)
        send(got, got, r_psib.at[1 + d], sibling)
        if d < downs:
            got = p_block(c, round_z(turn * (1 + d)))
            arrived(got, r_pdown.at[d])
            if d + 1 < downs:
                send(got, got, r_pdown.at[d + 1], z_last)
            send(got, got, r_psib.at[1 + ups + d], sibling)

    def p_sibling():
        zs = [z] + [round_z(turn * (1 + d)) for d in range(ups)] + [round_z(-turn * (1 + d)) for d in range(downs)]
        for k, zz in enumerate(zs):
            arrived(p_block(1 - c, zz), r_psib.at[k])

    def conv_inputs():
        for yy in others_y:
            arrived(edges.at[1 + yy], r_edge.at[yy])
        arrived(edges.at[1 + y], r_edge.at[y])
        rest(lambda yy: feat.at[yy], r_feat)
        for yy in range(ny):
            wide[8 : 8 + half_rows, :] = feat[yy].astype(F32)
            before, after = edges[yy + c].astype(F32), edges[yy + c + 1].astype(F32)
            for k in range(lanes // 128):
                wide[7:8, 128 * k : 128 * (k + 1)] = before[lanes // 128 + k : lanes // 128 + k + 1]
                wide[8 + half_rows : 9 + half_rows, 128 * k : 128 * (k + 1)] = after[k : k + 1]
            prev[yy] = wide[7 : 7 + half_rows, :].astype(BF)
            later[yy] = wide[9 : 9 + half_rows, :].astype(BF)

    for t in range(ups + 2):
        for j in range(count):
            if t == 0:
                w_start(j)
            if 0 < t <= ups:
                w_step(j, t - 1)
            if 1 < t:
                w_finish(j, t - 2)
        if t == 0:
            p_join()
        if t == 1:
            pass_on(lambda yy: feat.at[yy], r_feat)
        if t == P_START:
            p_start()
        if t > P_START:
            p_step(t - P_START - 1)
        if t == ups - 1:
            conv_inputs()

    cols = wc.shape[3]

    def dot(left, right):
        return jnp.dot(left, right, preferred_element_type=F32)

    def gelu(value, bias):
        value = value + bias
        inner = 0.7978845608028654 * (value + 0.044715 * (value * value * value))
        return value * (0.5 * (1.0 + jnp.tanh(inner)))

    def pool_part(part):
        return lambda yy: pool.at[yy, 2 * half_rows * part : 2 * half_rows * (part + 1)]

    def conv(part):
        def weight(first, last):
            return jnp.concatenate([wc[:, t].reshape(cin, cols) for t in range(first, last)], axis=0)

        bias = jnp.concatenate([bias_ref[pl.ds(y * (cols // 128) + k, 1), :] for k in range(cols // 128)], axis=1)
        yy = 2 * part

        def pair(ref):
            return ref[yy : yy + 2].reshape(2 * half_rows, lanes)

        before, now, after = pair(prev), pair(feat), pair(later)
        even = dot(before, weight(0, 2)) + dot(now, weight(2, 4)) + dot(after[:, :cin], weight(4, 5))
        odd = dot(before[:, cin:], weight(0, 1)) + dot(now, weight(1, 3)) + dot(after, weight(3, 5))
        value = jnp.maximum(gelu(even, bias), gelu(odd, bias)).astype(BF)
        pool[y, yy * half_rows : (yy + 2) * half_rows, :] = value

    for j in range(count):
        w_sibling(j)
    for part in range(ny // 2):
        conv(part)
        spread(pool_part(part)(y), pool_part(part)(y), r_pool.at[part])
    left = list(range(ups + 1 - P_START, ups))
    for part in range(ny // 2):
        pass_on(pool_part(part), r_pool.at[part])
        if left:
            p_step(left.pop(0))
    for d in left:
        p_step(d)
    p_sibling()

    for part in range(ny // 2):
        rest(pool_part(part), r_pool.at[part])
    width = ny * cols
    total = functools.reduce(
        jnp.add, [jnp.sum(pool[yy].astype(F32), axis=1, keepdims=True) for yy in range(ny)]
    )
    mean = total * (1.0 / width)
    square = functools.reduce(
        jnp.add, [jnp.sum(jnp.square(pool[yy].astype(F32) - mean), axis=1, keepdims=True) for yy in range(ny)]
    )
    inverse = 1.0 / jnp.sqrt(square * (1.0 / width) + 1e-05)

    def gain(yy):
        k = cols // 128
        return jnp.concatenate([gain_ref[yy * k + i : yy * k + i + 1, :] for i in range(k)], axis=1)

    acc = None
    for yy in range(ny):
        normed = ((pool[yy].astype(F32) - mean) * inverse * gain(yy)).astype(BF)
        part = dot(normed, pw[yy * cols : (yy + 1) * cols, :])
        acc = part if acc is None else acc + part
    qkv[c] = acc.astype(BF)
    send(qkv.at[c], qkv.at[c], r_kv.at[c], sibling)

    half = half_rows * ny // 2
    lane = lax.broadcasted_iota(jnp.int32, (half, 2 * HK), 1)
    wide_lane = lax.broadcasted_iota(jnp.int32, (half, cols), 1)

    def attend(side, first):
        rows_here = pl.ds(pl.multiple_of(side * half, half), half)
        query = qkv[c, rows_here, : 2 * HK]
        none = jnp.zeros_like(query)
        both = jnp.concatenate([jnp.where(lane < HK, query, none), jnp.where(lane < HK, none, query)], axis=0)

        def score(core):
            keys = qkv[core, :, 2 * HK : 4 * HK]
            return lax.dot_general(both, keys, (((1,), (1,)), ((), ())), preferred_element_type=F32) * (HK ** -0.5)

        here = score(c)
        if first:
            arrived(qkv.at[1 - c], r_kv.at[1 - c])
        there = score(1 - c)
        top = jnp.maximum(jnp.max(here, axis=1, keepdims=True), jnp.max(there, axis=1, keepdims=True))
        here, there = jnp.exp(here - top), jnp.exp(there - top)
        inv = 1.0 / (jnp.sum(here, axis=1, keepdims=True) + jnp.sum(there, axis=1, keepdims=True))
        result = dot((here * inv).astype(BF), qkv[c, :, 4 * HK :]) + dot((there * inv).astype(BF), qkv[1 - c, :, 4 * HK :])
        attended = jnp.where(wide_lane < HV, result[:half], result[half:]).astype(BF)
        total = (pool[y, rows_here, :].astype(F32) + attended.astype(F32)).astype(BF)
        mixed[pl.ds(side * (ny // 2), ny // 2)] = total.reshape(ny // 2, half_rows, cols)

    mine_side = lax.div(y, ny // 2)
    far = (1 - mine_side) * (ny // 2)
    attend(1 - mine_side, True)
    for k in range(ny // 2):
        send(mixed.at[far + k], landed.at[y], r_mix.at[y], at(h, z, x, far + k, c))
    attend(mine_side, False)
    near = mine_side * (ny // 2) + lax.rem(y + 1, 2)
    send(mixed.at[near], landed.at[y], r_mix.at[y], at(h, z, x, near, c))
    landed[y] = mixed[y]
    for yy in others_y:
        arrived(landed.at[yy], r_mix.at[yy])
    for yy in range(ny):
        out_ref[:, yy * cols : (yy + 1) * cols] = landed[yy]

    for cp, when in pending:
        if when is None:
            cp.wait_send()
        else:
            pl.when(when)(cp.wait_send)


def shards(features, conv_weight, conv_bias, norm_gain, qkv_weight):
    dp, ny = lax.axis_size("dp"), lax.axis_size("seq") // 2
    nx, nz = NX, dp // (NH * NX)
    taps, rows, cols = conv_weight.shape
    cols, cin, width = 2 * cols, rows * dp, 2 * ny * cols
    half_rows = features.shape[1] // 2
    step, heads = qkv_weight.shape
    heads = 2 * heads
    positions = half_rows * ny
    dma = pltpu.SemaphoreType.DMA
    vmem = pltpu.VMEM
    ups, downs = nz // 2, nz - 1 - nz // 2
    count = len(PARTS)
    strips = pl.cdiv(2 * 2 * cin // 128, 16) * 16
    packed, p_packed = pl.cdiv(taps * rows, 16) * 16, pl.cdiv(step, 16) * 16
    sends = 4 + (ny - 1) + 1 + ny + 2 * (nx - 1) + count * (3 * nz - 2) + 2 * ny + (2 * nz - 1) + 1 + (ny - 1)
    scratch = [
        vmem(features.shape[1:], BF),
        vmem(conv_weight.shape, BF),
        vmem((width // 128, 128), F32),
        vmem((width // 128, 128), F32),
        vmem(qkv_weight.shape, BF),
        vmem((half_rows, 2 * cin), BF),
        vmem((ny, half_rows, 2 * cin), BF),
        vmem((strips, 128), BF),
        vmem((ny + 2, strips, 128), BF),
        vmem((cin // 128, 2 * half_rows, 128), F32),
        vmem((half_rows + 16, 2 * cin), F32),
        vmem((ny, half_rows, 2 * cin), BF),
        vmem((ny, half_rows, 2 * cin), BF),
        vmem((packed, 256), F32),
        vmem((packed, 256), BF),
        vmem((2, packed, 256), BF),
        vmem((nx, packed, cols), BF),
        vmem((packed, cols), F32),
        vmem((taps, nx * rows, cols), F32),
        vmem((2 * nz, taps, nx * rows, cols), BF),
        vmem((p_packed, 384), BF),
        vmem((2, p_packed, 384), BF),
        vmem((nx, p_packed, heads), BF),
        vmem((nx * step, heads), F32),
        vmem((width, heads), BF),
        vmem((ny, positions, cols), BF),
        vmem((2, positions, heads), BF),
        vmem((ny, half_rows, cols), BF),
        vmem((ny, half_rows, cols), BF),
        dma((5,)), dma((sends,)), dma((ny,)), dma((ny,)), dma((2,)), dma((2,)), dma((nx,)), dma((nx,)),
        dma((count, ups)), dma((count, max(downs, 1))),
        dma((count, nz)), dma((ups,)), dma((max(downs, 1),)), dma((nz,)),
        dma((ny // 2, ny)), dma((2,)), dma((ny,)),
    ]
    out = pl.pallas_call(
        functools.partial(kernel, nz, nx, ny),
        out_shape=jax.ShapeDtypeStruct((half_rows, width), BF),
        in_specs=[pl.BlockSpec(memory_space=pltpu.HBM)] * 5,
        out_specs=pl.BlockSpec(memory_space=pltpu.VMEM),
        scratch_shapes=scratch,
        compiler_params=pltpu.CompilerParams(
            collective_id=0, has_side_effects=True, vmem_limit_bytes=64 * 2**20
        ),
        name="section",
    )(
        features[0],
        conv_weight,
        conv_bias.reshape(width // 128, 128),
        norm_gain.reshape(width // 128, 128),
        qkv_weight,
    )
    return out[None]


def solution(mesh):
    return jax.shard_map(
        shards,
        mesh=mesh,
        in_specs=(P("dp", "seq", None), P(None, "dp", "seq"), P(), P(), P("dp", "seq")),
        out_specs=P("dp", "seq", None),
        check_vma=False,
    )
```

time: 464 us -> 73.8 us (0.16)
  the two profiles are of different devices: /device:TPU:1 before, /device:TPU:59 now
where the time goes in v3:
time: 73.8 us; the launch traced here: 73.6 us
  Pallas kernels  72 us (98%)
  local copies, waits for them, and re-layouts  1.62 us (2%)
    pallas_call x1, Pallas kernels, shards(): pl.pallas_call(functools.partial(kernel, nz, nx, ny), out_shape=jax.Shape...  72 us
    unnamed x1, local copies, waits for them, and re-layouts  1.62 us

profile of v3, /device:TPU:59, one launch (start us, length us, event | category | flops | bytes accessed | tf_op | source)
XLA Modules:
  0.0 73.6 jit_solution(2923449224540172598)
XLA Ops:
  0.0 72.0 %section.1 = bf16[64,1536]{1,0:T(8,128)(2,1)} custom-call(bf16[128,768]{1,0:T(8,128)(2,1)} %bitcast.5, bf16[5,12,192]{2,1,0:T(8,128)(2,1)} %conv_in.1, f32[12,128]{1,0:T(8,128)} %bitcast.6, f32[12,128]{1,0:T(8,128)} %bitcast.7, bf16[24,320]{1,0:T(8,128)(2,1)} %proj_in.1), custom_call_target="tpu_custom_call" | custom-call | tf_op jit(solution)/shard_map/section/pallas_call | solution.py:466
  72.0 1.6 %copy.7 = bf16[1,64,1536]{2,1,0:T(8,128)(2,1)} copy(bf16[1,64,1536]{2,1,0:T(8,128)(2,1)} %bitcast.4) | data formatting | bytes 393216

commit v4 on v3

--- a/solution.py
+++ b/solution.py
@@ -13,8 +13,9 @@
 NX = 4
 BF = jnp.bfloat16
 F32 = jnp.float32
-P_START = 3
-PARTS = ((0, 2), (2, 2), (4, 1))
+LAG = 3
+GROUP = 128
+STAGGER = 0
 
 
 def kernel(
@@ -25,7 +26,7 @@
     wpack, wown, w0, w1, wflat32, wbuild, wc, pown, p0, p1, pbuild, pw,
     pool, qkv, mixed, landed,
     in_sems, send_sems, r_feat, r_edge, r_w0, r_p0, r_w1, r_p1,
-    r_wa, r_wb, r_wsib, r_pup, r_pdown, r_psib, r_pool, r_kv, r_mix,
+    r_wa, r_wb, r_wsib, r_pool, r_kv, r_mix,
 ):
     dp, seq = lax.axis_index("dp"), lax.axis_index("seq")
     h, z, x = lax.div(dp, nz * nx), lax.rem(lax.div(dp, nx), nz), lax.rem(dp, nx)
@@ -157,13 +158,10 @@
     w_rows = rows * nx
     p_rows = p_in * nx
     ups, downs = nz // 2, nz - 1 - nz // 2
-    count = len(PARTS)
+    count = wc.shape[0]
 
     def carried(distance):
         return lax.rem(z + x + c + distance, 2) == 0
-
-    def p_block(cc, zz):
-        return pw.at[pl.ds(pl.multiple_of((cc * nz + zz) * p_rows, 16), p_rows), :]
 
     for xx in others_x:
         arrived(w1.at[xx], r_w1.at[xx])
@@ -171,11 +169,13 @@
         wflat32[...] = w1[xx].astype(F32)
         for t in range(taps):
             wbuild[t, rows * xx : rows * (xx + 1), :] = wflat32[rows * t : rows * (t + 1), :]
-    wc[c * nz + z] = wbuild[...].astype(BF)
+    for j in range(count):
+        wc[j, c * nz + z] = wbuild[:, :, GROUP * j : GROUP * (j + 1)].astype(BF)
 
     def w_block(j, cc, zz):
-        tap, size = PARTS[j]
-        return wc.at[cc * nz + zz, tap : tap + size]
+        if j == count:
+            return pw.at[pl.ds(pl.multiple_of((cc * nz + zz) * p_rows, 16), p_rows), :]
+        return wc.at[j, cc * nz + zz]
 
     to_sibling = {}
 
@@ -202,6 +202,8 @@
 
             if d + 1 < steps:
                 send(block, block, recv.at[j, d + 1], z_to, carried(1 + d))
+        for zz, recv, steps, z_to, x_to, k in ways(d):
+            block = w_block(j, c, zz)
             send(block, block, recv.at[j, d], x_to, carried(1 + d))
             cp = copy(block, block, r_wsib.at[j, k], sibling, len(pending))
             pl.when(carried(1 + d))(cp.start)
@@ -241,29 +243,15 @@
         for xx in range(nx):
             pbuild[p_in * xx : p_in * (xx + 1), :] = p1[xx].astype(F32)[:p_in]
         pw[pl.ds(pl.multiple_of((c * nz + z) * p_rows, 16), p_rows), :] = pbuild[...].astype(BF)
-        block = p_block(c, z)
-        send(block, block, r_pup.at[0], z_next)
-        if downs:
-            send(block, block, r_pdown.at[0], z_last)
-        send(block, block, r_psib.at[0], sibling)
-
-    def p_step(d):
-        got = p_block(c, round_z(-turn * (1 + d)))
-        arrived(got, r_pup.at[d])
-        if d + 1 < ups:
-            send(got, got, r_pup.at[d + 1], z_next)
-        send(got, got, r_psib.at[1 + d], sibling)
-        if d < downs:
-            got = p_block(c, round_z(turn * (1 + d)))
-            arrived(got, r_pdown.at[d])
-            if d + 1 < downs:
-                send(got, got, r_pdown.at[d + 1], z_last)
-            send(got, got, r_psib.at[1 + ups + d], sibling)
-
-    def p_sibling():
-        zs = [z] + [round_z(turn * (1 + d)) for d in range(ups)] + [round_z(-turn * (1 + d)) for d in range(downs)]
-        for k, zz in enumerate(zs):
-            arrived(p_block(1 - c, zz), r_psib.at[k])
+        w_start(count)
+
+    def p_slot(k):
+        if k == 0:
+            p_start()
+        if 0 < k <= ups:
+            w_step(count, k - 1)
+        if 1 < k <= ups + 1:
+            w_finish(count, k - 2)
 
     def conv_inputs():
         for yy in others_y:
@@ -279,26 +267,25 @@
             prev[yy] = wide[7 : 7 + half_rows, :].astype(BF)
             later[yy] = wide[9 : 9 + half_rows, :].astype(BF)
 
-    for t in range(ups + 2):
+    for t in range(ups + 2 + STAGGER * (count - 1)):
         for j in range(count):
-            if t == 0:
+            k = t - STAGGER * j
+            if k == 0:
                 w_start(j)
-            if 0 < t <= ups:
-                w_step(j, t - 1)
-            if 1 < t:
-                w_finish(j, t - 2)
+            if 0 < k <= ups:
+                w_step(j, k - 1)
+            if 1 < k <= ups + 1:
+                w_finish(j, k - 2)
         if t == 0:
             p_join()
         if t == 1:
             pass_on(lambda yy: feat.at[yy], r_feat)
-        if t == P_START:
-            p_start()
-        if t > P_START:
-            p_step(t - P_START - 1)
+        if t >= LAG and t - LAG < ups + 2:
+            p_slot(t - LAG)
         if t == ups - 1:
             conv_inputs()
 
-    cols = wc.shape[3]
+    cols = count * GROUP
 
     def dot(left, right):
         return jnp.dot(left, right, preferred_element_type=F32)
@@ -308,48 +295,51 @@
         inner = 0.7978845608028654 * (value + 0.044715 * (value * value * value))
         return value * (0.5 * (1.0 + jnp.tanh(inner)))
 
-    def pool_part(part):
-        return lambda yy: pool.at[yy, 2 * half_rows * part : 2 * half_rows * (part + 1)]
-
-    def conv(part):
-        def weight(first, last):
-            return jnp.concatenate([wc[:, t].reshape(cin, cols) for t in range(first, last)], axis=0)
-
-        bias = jnp.concatenate([bias_ref[pl.ds(y * (cols // 128) + k, 1), :] for k in range(cols // 128)], axis=1)
-        yy = 2 * part
-
-        def pair(ref):
-            return ref[yy : yy + 2].reshape(2 * half_rows, lanes)
-
-        before, now, after = pair(prev), pair(feat), pair(later)
-        even = dot(before, weight(0, 2)) + dot(now, weight(2, 4)) + dot(after[:, :cin], weight(4, 5))
-        odd = dot(before[:, cin:], weight(0, 1)) + dot(now, weight(1, 3)) + dot(after, weight(3, 5))
-        value = jnp.maximum(gelu(even, bias), gelu(odd, bias)).astype(BF)
-        pool[y, yy * half_rows : (yy + 2) * half_rows, :] = value
-
+    def pool_part(j):
+        return lambda yy: pool.at[yy, j]
+
+    def whole(yy, rows_here=slice(None)):
+        return jnp.concatenate([pool[yy, j, rows_here, :].astype(F32) for j in range(count)], axis=1)
+
+    def conv(j):
+        bias = bias_ref[pl.ds(y * (cols // 128) + j, 1), :]
+
+        def flat(ref):
+            return ref[...].reshape(ny * half_rows, lanes)
+
+        before, now, after = flat(prev), flat(feat), flat(later)
+        taken = [before[:, :cin], before[:, cin:], now[:, :cin], now[:, cin:], after[:, :cin], after[:, cin:]]
+        total = None
+        for t in range(taps):
+            part_sum = dot(jnp.concatenate([taken[t], taken[t + 1]], axis=0), wc[j, :, t].reshape(cin, GROUP))
+            total = part_sum if total is None else total + part_sum
+        even, odd = total[: ny * half_rows], total[ny * half_rows :]
+        pool[y, j] = jnp.maximum(gelu(even, bias), gelu(odd, bias)).astype(BF)
+
+    left = list(range(max(ups + 2 + STAGGER * (count - 1) - LAG, 0), ups + 2))
     for j in range(count):
         w_sibling(j)
-    for part in range(ny // 2):
-        conv(part)
-        spread(pool_part(part)(y), pool_part(part)(y), r_pool.at[part])
-    left = list(range(ups + 1 - P_START, ups))
-    for part in range(ny // 2):
-        pass_on(pool_part(part), r_pool.at[part])
+        conv(j)
+        spread(pool_part(j)(y), pool_part(j)(y), r_pool.at[j])
+        if left and j:
+            p_slot(left.pop(0))
+    for j in range(count):
+        pass_on(pool_part(j), r_pool.at[j])
         if left:
-            p_step(left.pop(0))
-    for d in left:
-        p_step(d)
-    p_sibling()
-
-    for part in range(ny // 2):
-        rest(pool_part(part), r_pool.at[part])
+            p_slot(left.pop(0))
+    for k in left:
+        p_slot(k)
+    w_sibling(count)
+
+    for j in range(count):
+        rest(pool_part(j), r_pool.at[j])
     width = ny * cols
     total = functools.reduce(
-        jnp.add, [jnp.sum(pool[yy].astype(F32), axis=1, keepdims=True) for yy in range(ny)]
+        jnp.add, [jnp.sum(whole(yy), axis=1, keepdims=True) for yy in range(ny)]
     )
     mean = total * (1.0 / width)
     square = functools.reduce(
-        jnp.add, [jnp.sum(jnp.square(pool[yy].astype(F32) - mean), axis=1, keepdims=True) for yy in range(ny)]
+        jnp.add, [jnp.sum(jnp.square(whole(yy) - mean), axis=1, keepdims=True) for yy in range(ny)]
     )
     inverse = 1.0 / jnp.sqrt(square * (1.0 / width) + 1e-05)
 
@@ -359,7 +349,7 @@
 
     acc = None
     for yy in range(ny):
-        normed = ((pool[yy].astype(F32) - mean) * inverse * gain(yy)).astype(BF)
+        normed = ((whole(yy) - mean) * inverse * gain(yy)).astype(BF)
         part = dot(normed, pw[yy * cols : (yy + 1) * cols, :])
         acc = part if acc is None else acc + part
     qkv[c] = acc.astype(BF)
@@ -388,7 +378,7 @@
         inv = 1.0 / (jnp.sum(here, axis=1, keepdims=True) + jnp.sum(there, axis=1, keepdims=True))
         result = dot((here * inv).astype(BF), qkv[c, :, 4 * HK :]) + dot((there * inv).astype(BF), qkv[1 - c, :, 4 * HK :])
         attended = jnp.where(wide_lane < HV, result[:half], result[half:]).astype(BF)
-        total = (pool[y, rows_here, :].astype(F32) + attended.astype(F32)).astype(BF)
+        total = (whole(y, rows_here) + attended.astype(F32)).astype(BF)
         mixed[pl.ds(side * (ny // 2), ny // 2)] = total.reshape(ny // 2, half_rows, cols)
 
     mine_side = lax.div(y, ny // 2)
@@ -400,10 +390,15 @@
     near = mine_side * (ny // 2) + lax.rem(y + 1, 2)
     send(mixed.at[near], landed.at[y], r_mix.at[y], at(h, z, x, near, c))
     landed[y] = mixed[y]
-    for yy in others_y:
-        arrived(landed.at[yy], r_mix.at[yy])
-    for yy in range(ny):
-        out_ref[:, yy * cols : (yy + 1) * cols] = landed[yy]
+    writes = []
+    for i, yy in enumerate([y] + others_y):
+        if i:
+            arrived(landed.at[yy], r_mix.at[yy])
+        column = pl.multiple_of(yy * cols, 128)
+        writes.append(pltpu.make_async_copy(landed.at[yy], out_ref.at[:, pl.ds(column, cols)], in_sems.at[i]))
+        writes[-1].start()
+    for write in writes:
+        write.wait()
 
     for cp, when in pending:
         if when is None:
@@ -424,10 +419,10 @@
     dma = pltpu.SemaphoreType.DMA
     vmem = pltpu.VMEM
     ups, downs = nz // 2, nz - 1 - nz // 2
-    count = len(PARTS)
+    count = cols // GROUP
     strips = pl.cdiv(2 * 2 * cin // 128, 16) * 16
     packed, p_packed = pl.cdiv(taps * rows, 16) * 16, pl.cdiv(step, 16) * 16
-    sends = 4 + (ny - 1) + 1 + ny + 2 * (nx - 1) + count * (3 * nz - 2) + 2 * ny + (2 * nz - 1) + 1 + (ny - 1)
+    sends = 4 + (ny - 1) + 1 + ny + 2 * (nx - 1) + (count + 1) * (3 * nz - 2) + count * ny + 1 + (ny - 1)
     scratch = [
         vmem(features.shape[1:], BF),
         vmem(conv_weight.shape, BF),
@@ -448,26 +443,25 @@
         vmem((nx, packed, cols), BF),
         vmem((packed, cols), F32),
         vmem((taps, nx * rows, cols), F32),
-        vmem((2 * nz, taps, nx * rows, cols), BF),
+        vmem((count, 2 * nz, taps, nx * rows, GROUP), BF),
         vmem((p_packed, 384), BF),
         vmem((2, p_packed, 384), BF),
         vmem((nx, p_packed, heads), BF),
         vmem((nx * step, heads), F32),
         vmem((width, heads), BF),
-        vmem((ny, positions, cols), BF),
+        vmem((ny, count, positions, GROUP), BF),
         vmem((2, positions, heads), BF),
         vmem((ny, half_rows, cols), BF),
         vmem((ny, half_rows, cols), BF),
         dma((5,)), dma((sends,)), dma((ny,)), dma((ny,)), dma((2,)), dma((2,)), dma((nx,)), dma((nx,)),
-        dma((count, ups)), dma((count, max(downs, 1))),
-        dma((count, nz)), dma((ups,)), dma((max(downs, 1),)), dma((nz,)),
-        dma((ny // 2, ny)), dma((2,)), dma((ny,)),
+        dma((count + 1, ups)), dma((count + 1, max(downs, 1))), dma((count + 1, nz)),
+        dma((count, ny)), dma((2,)), dma((ny,)),
     ]
     out = pl.pallas_call(
         functools.partial(kernel, nz, nx, ny),
         out_shape=jax.ShapeDtypeStruct((half_rows, width), BF),
         in_specs=[pl.BlockSpec(memory_space=pltpu.HBM)] * 5,
-        out_specs=pl.BlockSpec(memory_space=pltpu.VMEM),
+        out_specs=pl.BlockSpec(memory_space=pltpu.HBM),
         scratch_shapes=scratch,
         compiler_params=pltpu.CompilerParams(
             collective_id=0, has_side_effects=True, vmem_limit_bytes=64 * 2**20

time: 73.8 us -> 71.3 us (0.966)
  the two profiles are of different devices: /device:TPU:59 before, /device:TPU:1 now
where the time goes in v4:
time: 71.3 us; the launch traced here: 71.1 us
  Pallas kernels  69.5 us (97%)
  local copies, waits for them, and re-layouts  1.62 us (2%)
    pallas_call x1, Pallas kernels, shards(): pl.pallas_call(functools.partial(kernel, nz, nx, ny), out_shape=jax.Shape...  69.5 us
    unnamed x1, local copies, waits for them, and re-layouts  1.62 us

profile of v4, /device:TPU:1, one launch (start us, length us, event | category | flops | bytes accessed | tf_op | source)
XLA Modules:
  0.0 71.1 jit_solution(8065218614869795667)
XLA Ops:
  0.0 69.5 %section.1 = bf16[64,1536]{1,0:T(8,128)(2,1)} custom-call(bf16[128,768]{1,0:T(8,128)(2,1)} %bitcast.5, bf16[5,12,192]{2,1,0:T(8,128)(2,1)} %conv_in.1, f32[12,128]{1,0:T(8,128)} %bitcast.6, f32[12,128]{1,0:T(8,128)} %bitcast.7, bf16[24,320]{1,0:T(8,128)(2,1)} %proj_in.1), custom_call_target="tpu_custom_call" | custom-call | tf_op jit(solution)/shard_map/section/pallas_call | solution.py:460
  69.5 1.6 %copy.7 = bf16[1,64,1536]{2,1,0:T(8,128)(2,1)} copy(bf16[1,64,1536]{2,1,0:T(8,128)(2,1)} %bitcast.4) | data formatting | bytes 393216

commit v5 on v4

--- a/solution.py
+++ b/solution.py
@@ -323,10 +323,9 @@
         spread(pool_part(j)(y), pool_part(j)(y), r_pool.at[j])
         if left and j:
             p_slot(left.pop(0))
-    for j in range(count):
-        pass_on(pool_part(j), r_pool.at[j])
-        if left:
-            p_slot(left.pop(0))
+        if j:
+            pass_on(pool_part(j - 1), r_pool.at[j - 1])
+    pass_on(pool_part(count - 1), r_pool.at[count - 1])
     for k in left:
         p_slot(k)
     w_sibling(count)

time: 71.3 us -> 71 us (level)
  no operation moved by 1% of the time
where the time goes in v5:
time: 71 us; the launch traced here: 70.8 us
  Pallas kernels  69.2 us (97%)
  local copies, waits for them, and re-layouts  1.62 us (2%)
    pallas_call x1, Pallas kernels, shards(): pl.pallas_call(functools.partial(kernel, nz, nx, ny), out_shape=jax.Shape...  69.2 us
    unnamed x1, local copies, waits for them, and re-layouts  1.62 us

profile of v5, /device:TPU:1, one launch (start us, length us, event | category | flops | bytes accessed | tf_op | source)
XLA Modules:
  0.0 70.8 jit_solution(16379506001108974894)
XLA Ops:
  0.0 69.2 %section.1 = bf16[64,1536]{1,0:T(8,128)(2,1)} custom-call(bf16[128,768]{1,0:T(8,128)(2,1)} %bitcast.5, bf16[5,12,192]{2,1,0:T(8,128)(2,1)} %conv_in.1, f32[12,128]{1,0:T(8,128)} %bitcast.6, f32[12,128]{1,0:T(8,128)} %bitcast.7, bf16[24,320]{1,0:T(8,128)(2,1)} %proj_in.1), custom_call_target="tpu_custom_call" | custom-call | tf_op jit(solution)/shard_map/section/pallas_call | solution.py:459
  69.2 1.6 %copy.7 = bf16[1,64,1536]{2,1,0:T(8,128)(2,1)} copy(bf16[1,64,1536]{2,1,0:T(8,128)(2,1)} %bitcast.4) | data formatting | bytes 393216

commit v6 on v5

--- a/solution.py
+++ b/solution.py
@@ -66,7 +66,7 @@
     half_rows, lanes = mine.shape
     cin = lanes // 2
     for k in range(cin // 128):
-        ext[k] = feat_ref[:, 128 * k : 128 * (k + 1)].astype(F32)
+        ext[k, : 2 * half_rows] = feat_ref[:, 128 * k : 128 * (k + 1)].astype(F32)
         mine[:, 128 * k : 128 * (k + 1)] = ext[k, pl.ds(0, half_rows, stride=2), :].astype(BF)
         mine[:, cin + 128 * k : cin + 128 * (k + 1)] = ext[k, pl.ds(1, half_rows, stride=2), :].astype(BF)
     first = mine[0:16, :].astype(F32)[0:1]
@@ -432,7 +432,7 @@
         vmem((ny, half_rows, 2 * cin), BF),
         vmem((strips, 128), BF),
         vmem((ny + 2, strips, 128), BF),
-        vmem((cin // 128, 2 * half_rows, 128), F32),
+        vmem((cin // 128, 2 * half_rows + 8, 128), F32),
         vmem((half_rows + 16, 2 * cin), F32),
         vmem((ny, half_rows, 2 * cin), BF),
         vmem((ny, half_rows, 2 * cin), BF),

time: 71 us -> 71 us (level)
  no operation moved by 1% of the time
where the time goes in v6:
time: 71 us; the launch traced here: 70.8 us
  Pallas kernels  69.2 us (97%)
  local copies, waits for them, and re-layouts  1.62 us (2%)
    pallas_call x1, Pallas kernels, shards(): pl.pallas_call(functools.partial(kernel, nz, nx, ny), out_shape=jax.Shape...  69.2 us
    unnamed x1, local copies, waits for them, and re-layouts  1.62 us

profile of v6, /device:TPU:1, one launch (start us, length us, event | category | flops | bytes accessed | tf_op | source)
XLA Modules:
  0.0 70.8 jit_solution(5742467088863655156)
XLA Ops:
  0.0 69.2 %section.1 = bf16[64,1536]{1,0:T(8,128)(2,1)} custom-call(bf16[128,768]{1,0:T(8,128)(2,1)} %bitcast.5, bf16[5,12,192]{2,1,0:T(8,128)(2,1)} %conv_in.1, f32[12,128]{1,0:T(8,128)} %bitcast.6, f32[12,128]{1,0:T(8,128)} %bitcast.7, bf16[24,320]{1,0:T(8,128)(2,1)} %proj_in.1), custom_call_target="tpu_custom_call" | custom-call | tf_op jit(solution)/shard_map/section/pallas_call | solution.py:459
  69.2 1.6 %copy.7 = bf16[1,64,1536]{2,1,0:T(8,128)(2,1)} copy(bf16[1,64,1536]{2,1,0:T(8,128)(2,1)} %bitcast.4) | data formatting | bytes 393216
